TPU v7x, 32 devices: a whole 2x2x4 slice. The times are simulated.
32 devices in a mesh: groups: 2 (over x), blk: 16 (over z, y, core).
Axes of the slice: x: 2, y: 2, z: 4, core: 2. Of those that a mesh axis runs over, the one named last changes fastest.
Arguments:
- embeddings: bfloat16 [6144, 256], P(('groups', 'blk')), parts along dimension 0, may hold values from -12 to 12
- codebook: bfloat16 [16384, 256], P(('groups', 'blk')), parts along dimension 0, may hold values from -5 to 5
Outputs:
- codebook_shift: bfloat16 [16384, 256], P(('groups', 'blk')), parts along dimension 0
- occupancy: float32 [16384], P(('groups', 'blk')), parts along dimension 0
- soft_quantized: bfloat16 [6144, 256], P(('groups', 'blk')), parts along dimension 0
- row_lse: float32 [6144], P(('groups', 'blk')), parts along dimension 0
There are 2 independent parts, one for each index of `groups`. A program takes and returns all parts, laid end to end along the dimension named above; each array names one. Nothing has to cross between parts.
All inputs are finite; a program needn't handle non-finite values.
Results may differ from a plain program's by a relative error of at most 0.005.
Values may be sent and summed in bfloat16 or wider, within the bound.
No kernel may reach another device: no remote copies, remote signals or barrier semaphores. Data moves between devices by JAX's collectives and lax.ppermute only.
A program may use at most 64 MiB of HBM per device.

v0:
```python
import math
import jax
import jax.numpy as jnp
from jax import lax
from jax.sharding import PartitionSpec as P


def row_block():
    return 1024


def block_scores(rows_data, code_block, norm_term, sharpness):
    return (
        sharpness
        * jnp.einsum("rd,kd->rk", rows_data, code_block, preferred_element_type=jnp.float32)
        - norm_term[None, :]
    )


def stats_block(rows_data, code_blocks, norm_terms, sharpness):

    def stat_step(running, scanned):
        running_max, running_sum = running
        code_block, norm_term = scanned
        scores = block_scores(rows_data, code_block, norm_term, sharpness)
        new_max = jnp.maximum(running_max, jnp.max(scores, axis=1))
        running_sum = running_sum * jnp.exp(running_max - new_max) + jnp.sum(
            jnp.exp(scores - new_max[:, None]), axis=1
        )
        return ((new_max, running_sum), None)

    row_count = rows_data.shape[0]
    initial = (
        jnp.full((row_count,), -jnp.inf, dtype=jnp.float32),
        jnp.zeros((row_count,), jnp.float32),
    )
    final, ignored = lax.scan(stat_step, initial, (code_blocks, norm_terms))
    return final


def row_stats(rows_data, code_blocks, norm_terms, sharpness):
    count = rows_data.shape[0]
    size = row_block()
    blocks = rows_data.reshape(count // size, size, rows_data.shape[1])
    result = lax.map(lambda rows: stats_block(rows, code_blocks, norm_terms, sharpness), blocks)
    return (result[0].reshape(count), result[1].reshape(count))


def share_pass(rows_data, lse_rows, code_blocks, norm_terms, sharpness):
    count = rows_data.shape[0]
    width = rows_data.shape[1]
    size = row_block()
    row_blocks = rows_data.reshape(count // size, size, width)
    lse_blocks = lse_rows.reshape(count // size, size)
    block_count = code_blocks.shape[0]
    block_size = code_blocks.shape[1]
    k_dev = block_count * block_size

    def outer_step(totals, scanned):
        rows_here, lse_here = scanned

        def inner_step(rebuilt, inner):
            code_block, norm_term = inner
            scores = block_scores(rows_here, code_block, norm_term, sharpness)
            shares = jnp.exp(scores - lse_here[:, None]).astype(jnp.bfloat16)
            weighted = jnp.einsum(
                "rk,rd->kd", shares, rows_here, preferred_element_type=jnp.float32
            )
            masses = jnp.sum(shares, axis=0, dtype=jnp.float32)
            rebuilt = rebuilt + jnp.dot(shares, code_block, preferred_element_type=jnp.float32)
            return (rebuilt, (weighted, masses))

        start = jnp.zeros((size, width), jnp.float32)
        rebuilt, stacked = lax.scan(inner_step, start, (code_blocks, norm_terms))
        new_totals = (
            totals[0] + stacked[0].reshape(k_dev, width),
            totals[1] + stacked[1].reshape(k_dev),
        )
        return (new_totals, rebuilt)

    initial = (jnp.zeros((k_dev, width), jnp.float32), jnp.zeros((k_dev,), jnp.float32))
    totals, per_rows = lax.scan(outer_step, initial, (row_blocks, lse_blocks))
    return (per_rows.reshape(count, per_rows.shape[2]), totals[0], totals[1])


def on_device(embeddings, codebook):
    rows_dev = embeddings.shape[0]
    feature_width = embeddings.shape[1]
    k_dev = codebook.shape[0]
    sharpness = 3.0 / math.sqrt(feature_width)
    block_size = min(k_dev, 1024)
    block_count = k_dev // block_size
    code_blocks = codebook.reshape(block_count, block_size, feature_width)
    norm_terms = (
        0.5 * sharpness * jnp.sum(jnp.square(codebook.astype(jnp.float32)), axis=1)
    ).reshape(block_count, block_size)
    gathered = lax.all_gather(embeddings, "blk", axis=0, tiled=True)
    local_max, local_sum = row_stats(gathered, code_blocks, norm_terms, sharpness)
    global_max = lax.pmax(local_max.astype(jnp.bfloat16), "blk").astype(local_max.dtype)
    global_total = lax.psum(local_sum * jnp.exp(local_max - global_max), "blk")
    lse_all = global_max + jnp.log(global_total)
    rebuilt, weighted, masses = share_pass(gathered, lse_all, code_blocks, norm_terms, sharpness)
    own_rebuilt = lax.psum_scatter(rebuilt, "blk", scatter_dimension=0, tiled=True)
    soft_quantized = own_rebuilt.astype(jnp.bfloat16)
    prior_mass = rows_dev / k_dev
    codebook_shift = (
        (weighted - masses[:, None] * codebook.astype(jnp.float32)) / (masses[:, None] + prior_mass)
    ).astype(jnp.bfloat16)
    occupancy = masses * (k_dev / rows_dev)
    own_lse = lax.dynamic_slice_in_dim(lse_all, lax.axis_index("blk") * rows_dev, rows_dev, 0)
    return (codebook_shift, occupancy, soft_quantized, own_lse)


def solution(mesh):
    in_specs = (P(("groups", "blk"), None), P(("groups", "blk"), None))
    out_specs = (
        P(("groups", "blk"), None),
        P(("groups", "blk")),
        P(("groups", "blk"), None),
        P(("groups", "blk")),
    )
    return jax.shard_map(
        on_device, mesh=mesh, in_specs=in_specs, out_specs=out_specs, check_vma=False
    )
```

profile of v0, /device:TPU:0, one launch (start us, length us, event | category | flops | bytes accessed | tf_op | source)
XLA Modules:
  0.0 236.2 jit_solution(4751557155126825032)
XLA Ops:
  7.2 0.7 all-gather.2.cloned.1.call-update
  8.0 1.1 fusion.15
  9.1 43.6 %all-gather.2.cloned.1.call-done = bf16[3072,256]{1,0:T(8,128)(2,1)} async-done(((bf16[192,256]{1,0:T(8,128)(2,1)}), bf16[3072,256]{1,0:T(8,128)(2,1)}) %all-gather.2.cloned.1.call-update) | async-done | bytes 1572880 | tf_op jit(solution)/shard_map/all_gather | solution.py:97
  52.7 6.9 %while.27 = (s32[]{:T(128)}, f32[3,1024]{1,0:T(4,128)S(1)}, f32[3,1024]{1,0:T(4,128)S(1)}, bf16[3,1024,256]{2,1,0:T(8,128)(2,1)}, bf16[1,512,256]{2,1,0:T(8,128)...) while((s32[]{:T(128)}, f32[3,1024]{1,0:T(4,128)S(1)}, f32[3,1024]{1,0:T(4,128)S(1)}, ...), condition=%wide.region_4.5_spmd, body=%wide.region_1.4_spmd.sunk | while | flops 272106496 | bytes 5025897 | solution.py:45
  52.7 1.6 fusion.29
  54.3 0.5 exponential_reduce_fusion.2
  54.8 0.1 dynamic_update_slice.22
  54.9 0.1 dynamic_update_slice.23
  55.0 1.6 fusion.29
  56.6 0.5 exponential_reduce_fusion.2
  57.1 0.1 dynamic_update_slice.22
  57.2 0.1 dynamic_update_slice.23
  57.3 1.6 fusion.29
  58.9 0.5 exponential_reduce_fusion.2
  59.4 0.1 dynamic_update_slice.22
  59.6 32.1 %pmax.7 = bf16[3072]{0:T(1024)(128)(2,1)S(1)} all-reduce(bf16[3072]{0:T(1024)(128)(2,1)S(1)} %convert_element_type.25), channel_id=1, replica_groups=mesh['groups'=2,'blk'=16] {'blk'}, use_global_device_ids=true, to_apply=%region_5.6 | all-reduce | flops 3072 | bytes 12288 | tf_op jit(solution)/shard_map/pmax | solution.py:99
  91.7 57.6 %psum.7 = f32[3072]{0:T(1024)S(1)} all-reduce(f32[3072]{0:T(1024)S(1)} %fusion.20), channel_id=1, replica_groups=mesh['groups'=2,'blk'=16] {'blk'}, use_global_device_ids=true, to_apply=%region_6.7 | all-reduce | flops 3072 | bytes 24576 | tf_op jit(solution)/shard_map/psum | solution.py:100
  149.4 14.8 %while.28 = (s32[]{:T(128)}, f32[512,256]{1,0:T(8,128)S(1)}, f32[512]{0:T(512)S(1)}, f32[3,1024,256]{2,1,0:T(8,128)}, bf16[3,1024,256]{2,1,0:T(8,128)(2,1)}, /*i...) while((s32[]{:T(128)}, f32[512,256]{1,0:T(8,128)S(1)}, ...), condition=%wide.region_9.10_spmd.clone, body=%wide.region_7.9_spmd.clone.sunk | while | flops 808714752 | bytes 7887012 | solution.py:82
  149.4 1.8 convert_reduce_fusion.2
  151.2 1.7 convolution_add_fusion.2
  152.9 1.4 fusion.34
  154.3 1.8 convert_reduce_fusion.2
  156.1 1.7 convolution_add_fusion.2
  157.8 1.5 fusion.34
  159.3 1.8 convert_reduce_fusion.2
  161.1 1.7 convolution_add_fusion.2
  162.8 1.4 fusion.34
  164.2 0.6 dynamic_slice.24
  164.9 0.6 broadcast_multiply_fusion
  165.4 0.9 fusion.18
  166.4 61.4 %reduce-scatter.2.cloned.1.call-done = f32[192,256]{1,0:T(8,128)} async-done(((f32[3072,256]{1,0:T(8,128)}), f32[192,256]{1,0:T(8,128)}) %reduce-scatter.2.cloned.1.call-update) | async-done | bytes 196624 | tf_op jit(solution)/shard_map/reduce_scatter | solution.py:103
  227.8 1.6 convert_element_type.28
  (33 shorter events, 0.4 us)
Async XLA Ops:
  7.2 45.5 %all-gather.2.cloned.1.call-start = ((), (), s32[]{:S(2)}) async-start(), calls=%async_computation.1 | async-start | bytes 1671168 | tf_op jit(solution)/shard_map/all_gather | solution.py:97
  7.9 219.9 %reduce-scatter.2.cloned.1.call-start = ((), (), s32[]{:S(2)}) async-start(), calls=%async_computation.2 | async-start | bytes 3342336 | tf_op jit(solution)/shard_map/reduce_scatter | solution.py:103
  151.2 1.7 copy-start
  156.1 1.7 copy-start
  161.1 1.7 copy-start
  164.2 1.3 copy-start.1
Sparse Core Ops, SparseCore 0:
  10.3 42.3 all-gather.1
  164.3 63.4 reduce-scatter.1
where the time goes:
time: 237 us; the launch traced here: 236 us
  waiting for transfers between devices  106 us (45%)
  blocking collectives  89.7 us (38%)
  matrix products  19.4 us (8%)
  between operations  14.1 us (6%)
  other arithmetic  5.73 us (2%)
    reduce_scatter x1, waiting for transfers between devices, on_device(): lax.psum_scatter(rebuilt, 'blk', scatter_dimension=0, tiled=True)  61.4 us
    psum x1, blocking collectives, on_device(): global_total = lax.psum(local_sum * jnp.exp(local_max - global_max), 'blk')  57.6 us
    all_gather x1, waiting for transfers between devices, on_device(): gathered = lax.all_gather(embeddings, 'blk', axis=0, tiled=True)  43.6 us
    pmax x1, blocking collectives, on_device(): lax.pmax(local_max.astype(jnp.bfloat16), 'blk').astype(local_max.dtype)  32.1 us
    dot_general x6, matrix products, block_scores(): jnp.einsum('rd,kd->rk', rows_data, code_block, preferred_element_type=jnp...  10.1 us
    dot_general x3, matrix products, inner_step(): jnp.einsum('rk,rd->kd', shares, rows_here, preferred_element_type=jnp.flo...  4.99 us
  transfers between devices with their start and end apart: 2, of which 2 were waited for; matrix products, arithmetic and copies ran while one was open for 1% of the time, Pallas kernels for 0%

commit v1 on v0

--- a/solution.py
+++ b/solution.py
@@ -84,6 +84,11 @@
 
 
 def on_device(embeddings, codebook):
+
+    def teams_derive(inner_x, net_axis):
+        carry = jax.lax.all_gather(inner_x, net_axis)
+        return jnp.sum(carry, axis=0)
+
     rows_dev = embeddings.shape[0]
     feature_width = embeddings.shape[1]
     k_dev = codebook.shape[0]
@@ -97,7 +102,7 @@
     gathered = lax.all_gather(embeddings, "blk", axis=0, tiled=True)
     local_max, local_sum = row_stats(gathered, code_blocks, norm_terms, sharpness)
     global_max = lax.pmax(local_max.astype(jnp.bfloat16), "blk").astype(local_max.dtype)
-    global_total = lax.psum(local_sum * jnp.exp(local_max - global_max), "blk")
+    global_total = teams_derive(local_sum * jnp.exp(local_max - global_max), "blk")
     lse_all = global_max + jnp.log(global_total)
     rebuilt, weighted, masses = share_pass(gathered, lse_all, code_blocks, norm_terms, sharpness)
     own_rebuilt = lax.psum_scatter(rebuilt, "blk", scatter_dimension=0, tiled=True)

time: 237 us -> 198 us (0.84)
  blocking collectives: 89.7 us -> 49.8 us
    psum x1 -> x0, blocking collectives: 57.6 us -> none  [on_device(): global_total = lax.psum(local_sum * jnp.exp(local_max - global_max), 'blk')]
    all_gather x0 -> x1, blocking collectives: none -> 17.7 us  [teams_derive(): carry = jax.lax.all_gather(inner_x, net_axis)]
  transfers between devices with their start and end apart: 2 -> 2, of which waited for: 2 -> 2; matrix products, arithmetic and copies ran while one was open for 1% -> 2% of each run, Pallas kernels for 0% -> 0%
where the time goes in v1:
time: 198 us
  waiting for transfers between devices  107 us (54%)
  blocking collectives  49.8 us (25%)
  matrix products  19.4 us (10%)
  between operations  14.2 us (7%)
  other arithmetic  5.77 us (3%)
    reduce_scatter x1, waiting for transfers between devices, on_device(): lax.psum_scatter(rebuilt, 'blk', scatter_dimension=0, tiled=True)  63 us
    all_gather x1, waiting for transfers between devices, on_device(): gathered = lax.all_gather(embeddings, 'blk', axis=0, tiled=True)  43.6 us
    pmax x1, blocking collectives, on_device(): lax.pmax(local_max.astype(jnp.bfloat16), 'blk').astype(local_max.dtype)  32.1 us
    all_gather x1, blocking collectives, teams_derive(): carry = jax.lax.all_gather(inner_x, net_axis)  17.7 us
    dot_general x6, matrix products, block_scores(): jnp.einsum('rd,kd->rk', rows_data, code_block, preferred_element_type=jnp...  10.1 us
    dot_general x3, matrix products, inner_step(): jnp.einsum('rk,rd->kd', shares, rows_here, preferred_element_type=jnp.flo...  4.98 us
    dot_general x3, matrix products, inner_step(): jnp.dot(shares, code_block, preferred_element_type=jnp.float32)  4.33 us
  transfers between devices with their start and end apart: 2, of which 2 were waited for; matrix products, arithmetic and copies ran while one was open for 2% of the time, Pallas kernels for 0%

profile of v1, /device:TPU:0, one launch (start us, length us, event | category | flops | bytes accessed | tf_op | source)
XLA Modules:
  0.0 198.0 jit_solution(12839269115954113677)
XLA Ops:
  7.2 0.7 all-gather.3.cloned.1.call-update
  8.0 1.1 fusion.15
  9.1 43.6 %all-gather.3.cloned.1.call-done = bf16[3072,256]{1,0:T(8,128)(2,1)} async-done(((bf16[192,256]{1,0:T(8,128)(2,1)}), bf16[3072,256]{1,0:T(8,128)(2,1)}) %all-gather.3.cloned.1.call-update) | async-done | bytes 1572880 | tf_op jit(solution)/shard_map/all_gather | solution.py:102
  52.7 6.9 %while.27 = (s32[]{:T(128)}, f32[3,1024]{1,0:T(4,128)S(1)}, f32[3,1024]{1,0:T(4,128)S(1)}, bf16[3,1024,256]{2,1,0:T(8,128)(2,1)}, bf16[1,512,256]{2,1,0:T(8,128)...) while((s32[]{:T(128)}, f32[3,1024]{1,0:T(4,128)S(1)}, f32[3,1024]{1,0:T(4,128)S(1)}, ...), condition=%wide.region_4.5_spmd, body=%wide.region_1.4_spmd.sunk | while | flops 272106496 | bytes 5025897 | solution.py:45
  52.7 1.6 fusion.29
  54.3 0.5 exponential_reduce_fusion.2
  54.8 0.1 dynamic_update_slice.22
  54.9 0.1 dynamic_update_slice.23
  55.0 1.6 fusion.29
  56.6 0.5 exponential_reduce_fusion.2
  57.1 0.1 dynamic_update_slice.22
  57.2 0.1 dynamic_update_slice.23
  57.3 1.6 fusion.29
  58.9 0.5 exponential_reduce_fusion.2
  59.4 0.1 dynamic_update_slice.22
  59.6 32.1 %pmax.7 = bf16[3072]{0:T(1024)(128)(2,1)S(1)} all-reduce(bf16[3072]{0:T(1024)(128)(2,1)S(1)} %convert_element_type.25), channel_id=1, replica_groups=mesh['groups'=2,'blk'=16] {'blk'}, use_global_device_ids=true, to_apply=%region_5.6 | all-reduce | flops 3072 | bytes 12288 | tf_op jit(solution)/shard_map/pmax | solution.py:104
  91.7 17.7 %all-gather = f32[49152]{0:T(1024)S(1)} all-gather(f32[3072]{0:T(1024)S(1)} %fusion.20), channel_id=2, replica_groups=mesh['groups'=2,'blk'=16] {'blk'}, dimensions={0}, use_global_device_ids=true | all-gather | bytes 208896 | tf_op jit(solution)/shard_map/all_gather | solution.py:89
  109.5 14.8 %while.28 = (s32[]{:T(128)}, f32[512,256]{1,0:T(8,128)S(1)}, f32[512]{0:T(512)S(1)}, f32[3,1024,256]{2,1,0:T(8,128)}, bf16[3,1024,256]{2,1,0:T(8,128)(2,1)}, /*i...) while((s32[]{:T(128)}, f32[512,256]{1,0:T(8,128)S(1)}, ...), condition=%wide.region_9.10_spmd.clone, body=%wide.region_7.9_spmd.clone.sunk | while | flops 808714752 | bytes 7887012 | solution.py:82
  109.6 1.8 convert_reduce_fusion.2
  111.4 1.7 convolution_add_fusion.2
  113.0 1.4 fusion.34
  114.5 1.8 convert_reduce_fusion.2
  116.3 1.7 convolution_add_fusion.2
  118.0 1.5 fusion.34
  119.4 1.8 convert_reduce_fusion.2
  121.2 1.7 convolution_add_fusion.2
  122.9 1.4 fusion.34
  124.4 0.6 dynamic_slice.24
  125.0 0.6 broadcast_multiply_fusion
  125.6 0.9 fusion.18
  126.5 63.0 %reduce-scatter.2.cloned.1.call-done = f32[192,256]{1,0:T(8,128)} async-done(((f32[3072,256]{1,0:T(8,128)}), f32[192,256]{1,0:T(8,128)}) %reduce-scatter.2.cloned.1.call-update) | async-done | bytes 196624 | tf_op jit(solution)/shard_map/reduce_scatter | solution.py:108
  189.5 1.6 convert_element_type.28
  (35 shorter events, 0.4 us)
Async XLA Ops:
  7.2 45.5 %all-gather.3.cloned.1.call-start = ((), (), s32[]{:S(2)}) async-start(), calls=%async_computation.1 | async-start | bytes 1671168 | tf_op jit(solution)/shard_map/all_gather | solution.py:102
  7.9 181.6 %reduce-scatter.2.cloned.1.call-start = ((), (), s32[]{:S(2)}) async-start(), calls=%async_computation.2 | async-start | bytes 3342336 | tf_op jit(solution)/shard_map/reduce_scatter | solution.py:108
  111.3 1.7 copy-start
  116.2 1.7 copy-start
  121.2 1.7 copy-start
  124.3 1.3 copy-start.1
Sparse Core Ops, SparseCore 0:
  10.3 42.3 all-gather.2
  124.5 65.0 reduce-scatter.1
